TPU v7x, 256 devices: a whole 4x4x8 slice. The times are simulated.
256 devices in a mesh: dp: 2 (over y_hi), expert: 128 (over x, y_lo, z, core).
Axes of the slice: x: 4, y: 4 (y_hi: 2, y_lo: 2; y = y_hi * 2 + y_lo), z: 8, core: 2. Of those that a mesh axis runs over, the one named last changes fastest.
Arguments:
- tokens: bfloat16 [4096, 4096], P(('dp', 'expert')), may hold values from -6 to 6
- routing: int32 [4096, 2], P(('dp', 'expert')), may hold values from 0 to 7, as said below
- hidden_grad: bfloat16 [131072, 512], P(('dp', 'expert')), may hold values from -3 to 3
- gate_weight: bfloat16 [4096, 65536], P(None, 'expert'), may hold values from -0.09375 to 0.09375
- up_weight: bfloat16 [4096, 65536], P(None, 'expert'), may hold values from -0.09375 to 0.09375
Outputs:
- token_grad: bfloat16 [4096, 4096], P(('dp', 'expert'))
- gate_weight_grad: bfloat16 [4096, 65536], P('dp', 'expert')
- up_weight_grad: bfloat16 [4096, 65536], P('dp', 'expert')
Inputs may be any that keep to these rules, and one draw needn't show every extreme that they name: `routing`: the 2 entries of a token differ, and no device names one expert in more than 4 of its tokens.
All inputs are finite; a program needn't handle non-finite values.
Results may differ from a plain program's by a relative error of at most 0.0085.
Values may be sent and summed in bfloat16 or wider, within the bound.
No kernel may reach another device: no remote copies, remote signals or barrier semaphores. Data moves between devices by JAX's collectives and lax.ppermute only.
A program may use at most 128 MiB of HBM per device.

v0:
```python
import jax
import jax.numpy as jnp
from jax import lax
from jax.sharding import Mesh, PartitionSpec as P

EXPERTS = 8
TOP = 2
CAP = 4


def slot_tables(routing_dev):
    flat_experts = routing_dev.reshape(-1)
    onehot = (flat_experts[:, None] == jnp.arange(EXPERTS, dtype=jnp.int32)[None, :]).astype(
        jnp.int32
    )
    before = jnp.cumsum(onehot, axis=0) - onehot
    slot_index = jnp.sum(before * onehot, axis=1)
    target = flat_experts * CAP + slot_index
    placed = target[:, None] == jnp.arange(EXPERTS * CAP, dtype=jnp.int32)[None, :]
    return placed.astype(jnp.float32)


def contract_rows(left_rows, right_rows):
    return lax.dot_general(
        left_rows, right_rows, (((0,), (0,)), ((), ())), preferred_element_type=jnp.float32
    )


def swap_dp(block):
    return lax.ppermute(block, "dp", [(0, 1), (1, 0)])


def per_device(tokens, routing, hidden_grad, gate_weight, up_weight):
    token_count, model_width = tokens.shape
    ffd = gate_weight.shape[1]
    shards = lax.axis_size("s")
    half = model_width // 2
    replica = lax.axis_index("dp")
    placed = slot_tables(routing)
    chosen = jnp.sum(placed.reshape(token_count, TOP, EXPERTS * CAP), axis=1)
    outgoing = lax.dot_general(
        chosen.astype(jnp.bfloat16),
        tokens,
        (((0,), (0,)), ((), ())),
        preferred_element_type=jnp.float32,
    ).astype(jnp.bfloat16)
    mine = lax.all_to_all(
        outgoing.reshape(EXPERTS, CAP, model_width), "e", split_axis=0, concat_axis=0, tiled=True
    ).reshape(EXPERTS * CAP, model_width)
    far_mine = swap_dp(lax.dynamic_slice_in_dim(mine, (1 - replica) * half, half, 1))
    rows = lax.all_gather(mine, "s", axis=0, tiled=True)
    far_rows = lax.all_gather(far_mine, "s", axis=0, tiled=True)
    grad_h = (
        hidden_grad.reshape(EXPERTS, shards, CAP, ffd)
        .transpose(1, 0, 2, 3)
        .reshape(-1, ffd)
        .astype(jnp.float32)
    )
    gate_pre = jnp.dot(rows, gate_weight, preferred_element_type=jnp.float32)
    up_pre = jnp.dot(rows, up_weight, preferred_element_type=jnp.float32)
    sig = jax.nn.sigmoid(gate_pre)
    gate_grad = (grad_h * up_pre * sig * (1.0 + gate_pre * (1.0 - sig))).astype(jnp.bfloat16)
    up_grad = (grad_h * gate_pre * sig).astype(jnp.bfloat16)
    grads = jnp.concatenate([gate_grad, up_grad], axis=1)
    far_grads = swap_dp(grads)
    transposed = (((1,), (1,)), ((), ()))
    partial_value = lax.dot_general(
        gate_grad, gate_weight, transposed, preferred_element_type=jnp.float32
    )
    partial_value = partial_value + lax.dot_general(
        up_grad, up_weight, transposed, preferred_element_type=jnp.float32
    )
    partial_value = partial_value.astype(jnp.bfloat16)
    summed = lax.psum_scatter(partial_value, "s", scatter_dimension=0, tiled=True)
    back = lax.all_to_all(
        summed.reshape(EXPERTS, CAP, model_width), "e", split_axis=0, concat_axis=0, tiled=True
    ).reshape(EXPERTS * CAP, model_width)
    token_grad = jnp.dot(
        chosen.astype(jnp.bfloat16), back, preferred_element_type=jnp.float32
    ).astype(jnp.bfloat16)
    own_columns = lax.dynamic_slice_in_dim(rows, replica * half, half, 1)
    own_term = lax.optimization_barrier(contract_rows(own_columns, grads).astype(jnp.bfloat16))
    weight_sum = own_term.astype(jnp.float32) + contract_rows(far_rows, far_grads)
    return (
        token_grad,
        weight_sum[:, :ffd].astype(jnp.bfloat16),
        weight_sum[:, ffd:].astype(jnp.bfloat16),
    )


def solution(mesh):
    n_dp, n_expert = mesh.devices.shape
    fine = Mesh(mesh.devices.reshape(n_dp, EXPERTS, n_expert // EXPERTS), ("dp", "e", "s"))
    all_axes = ("dp", "e", "s")
    in_specs = (
        P(all_axes, None),
        P(all_axes, None),
        P(all_axes, None),
        P(None, ("e", "s")),
        P(None, ("e", "s")),
    )
    out_specs = (P(all_axes, None), P("dp", ("e", "s")), P("dp", ("e", "s")))
    return jax.shard_map(
        per_device, mesh=fine, in_specs=in_specs, out_specs=out_specs, check_vma=False
    )
```

profile of v0, /device:TPU:16, one launch (start us, length us, event | category | flops | bytes accessed | tf_op | source)
XLA Modules:
  0.0 191.4 jit_solution(17602063873971808503)
XLA Ops:
  7.2 0.0 copy-start
  7.2 0.0 all-gather.3.cloned.1.call-start
  7.2 0.8 copy.25
  8.0 0.1 eq.29
  8.1 0.1 fusion.4
  8.2 0.1 reduce_window_sum.11
  8.2 0.2 select_reduce_fusion
  8.4 0.1 reduce_sum.21
  8.5 0.1 copy.26
  8.6 0.7 multiply_add_fusion
  9.3 0.1 convert_reduce_fusion
  9.4 0.0 copy-done
  9.4 0.2 convolution_convert_fusion
  9.6 0.1 reshape.43
  9.7 12.0 %all_to_all.10 = bf16[8,4,4096]{2,1,0:T(4,128)(2,1)S(1)} all-to-all(bf16[8,4,4096]{2,1,0:T(4,128)(2,1)S(1)} %reshape.43), channel_id=1, replica_groups=mesh['dp'=2,'e'=8,'s'=16] {'e'}, dimensions={0} | all-to-all | bytes 524288 | tf_op jit(solution)/shard_map/all_to_all | solution.py:47
  21.8 0.8 reshape.44
  22.5 0.0 all-gather.3.cloned.1.call-update
  22.6 0.0 all-gather.5.cloned.1.call-start
  22.6 0.9 constant_dynamic-slice_fusion
  23.5 0.7 collective-permute-start
  24.2 5.8 %collective-permute-done = bf16[32,2048]{1,0:T(8,128)(2,1)S(1)} collective-permute-done((bf16[32,2048]{1,0:T(8,128)(2,1)S(1)}, bf16[32,2048]{1,0:T(8,128)(2,1)S(1)}, u32[]{:S(2)}, u32[]{:S(2)}) %collective-permute-start) | collective-permute-done | bytes 131104 | tf_op jit(solution)/shard_map/ppermute | solution.py:30
  30.1 0.7 copy-done.3
  30.7 0.0 all-gather.5.cloned.1.call-update
  30.8 0.0 reduce-scatter.2.cloned.1.call-start
  30.8 1.4 reshape.48
  32.2 0.1 copy.31
  32.3 0.4 reshape.47
  32.7 0.3 copy.28
  33.0 32.5 %all-gather.3.cloned.1.call-done = bf16[512,4096]{1,0:T(8,128)(2,1)} async-done(((bf16[32,4096]{1,0:T(8,128)(2,1)}), bf16[512,4096]{1,0:T(8,128)(2,1)}) %all-gather.3.cloned.1.call-update) | async-done | bytes 4194320 | tf_op jit(solution)/shard_map/all_gather | solution.py:51
  65.5 6.1 %multiply_convert_fusion = (bf16[512,512]{0,1:T(8,128)(2,1)S(1)}, f32[512,512]{0,1:T(8,128)S(1)}) fusion(f32[512,512]{0,1:T(8,128)S(1)} %copy.28, bf16[512,4096]{1,0:T(8,128)(2,1)} %all-gather.3.cloned.1.call-done, bf16[4096,512]{1,0:T(8,128)(2,1)} %param.8), kind=kOutput, calls=%fused_computation.12 | convolution fusion | flops 2149056512 | bytes 11010048 | tf_op jit(solution)/shard_map/dot_general | solution.py:59
  71.7 0.0 copy-start.1
  71.7 2.6 %fusion.3 = bf16[512,512]{0,1:T(8,128)(2,1)S(1)} fusion(f32[512,512]{0,1:T(8,128)S(1)} %copy.28, bf16[512,4096]{1,0:T(8,128)(2,1)S(1)} %copy-done.4, bf16[4096,512]{1,0:T(8,128)(2,1)S(1)} %copy-done.2, f32[512,512]{0,1:T(8,128)S(1)} %get-tuple-element.6), kind=kOutput, calls=%fused_computation.9 | convolution fusion | flops 2150105088 | bytes 11010048 | tf_op jit(solution)/shard_map/dot_general | solution.py:60
  74.3 2.4 %fusion.9 = f32[512,4096]{1,0:T(8,128)S(1)} fusion(bf16[512,512]{0,1:T(8,128)(2,1)S(1)} %fusion.3, bf16[4096,512]{1,0:T(8,128)(2,1)S(1)} %copy-done.1), kind=kOutput, calls=%fused_computation.25 | convolution fusion | flops 2147483648 | bytes 13107200 | tf_op jit(solution)/shard_map/dot_general | solution.py:67
  76.8 4.5 %add_convert_fusion.1 = bf16[512,4096]{1,0:T(8,128)(2,1)} fusion(f32[512,4096]{1,0:T(8,128)S(1)} %fusion.9, bf16[512,512]{0,1:T(8,128)(2,1)S(1)} %get-tuple-element.5, bf16[4096,512]{1,0:T(8,128)(2,1)S(1)} %copy-done.2), kind=kOutput, calls=%fused_computation.1 | convolution fusion | flops 2151677952 | bytes 17301504 | tf_op jit(solution)/shard_map/dot_general | solution.py:70
  81.2 0.0 reduce-scatter.2.cloned.1.call-update
  81.2 0.1 pad_maximum_fusion
  81.3 0.8 collective-permute-start.1
  82.1 6.0 %convolution_convert_fusion.2 = bf16[2048,1024]{1,0:T(8,128)(2,1)} fusion(bf16[512,4096]{1,0:T(8,128)(2,1)} %all-gather.3.cloned.1.call-done, s32[]{:T(128)S(6)} %select_n.6, bf16[512,512]{0,1:T(8,128)(2,1)S(1)} %get-tuple-element.5, bf16[512,512]{0,1:T(8,128)(2,1)S(1)} %fusion.3), kind=kOutput, calls=%fused_computation.4 | convolution fusion | flops 2151677952 | bytes 7340036 | tf_op jit(solution)/shard_map/dot_general | solution.py:24
  88.1 17.9 %all-gather.5.cloned.1.call-done = bf16[512,2048]{1,0:T(8,128)(2,1)} async-done(((bf16[32,2048]{1,0:T(8,128)(2,1)}), bf16[512,2048]{1,0:T(8,128)(2,1)}) %all-gather.5.cloned.1.call-update) | async-done | bytes 2097168 | tf_op jit(solution)/shard_map/all_gather | solution.py:52
  106.0 2.4 %collective-permute-done.1 = bf16[512,1024]{0,1:T(8,128)(2,1)S(1)} collective-permute-done((bf16[512,1024]{0,1:T(8,128)(2,1)S(1)}, bf16[512,1024]{0,1:T(8,128)(2,1)S(1)}, u32[]{:S(2)}, u32[]{:S(2)}) %collective-permute-start.1) | collective-permute-done | bytes 1048608 | tf_op jit(solution)/shard_map/ppermute | solution.py:30
  108.4 7.2 %add_convert_fusion = bf16[2048,1024]{1,0:T(8,128)(2,1)} fusion(bf16[2048,1024]{1,0:T(8,128)(2,1)} %convolution_convert_fusion.2, bf16[512,2048]{1,0:T(8,128)(2,1)} %all-gather.5.cloned.1.call-done, bf16[512,1024]{0,1:T(8,128)(2,1)S(1)} %collective-permute-done.1), kind=kOutput, calls=%fused_computation | convolution fusion | flops 2153775104 | bytes 11534336 | tf_op jit(solution)/shard_map/dot_general | solution.py:24
  115.6 54.6 %reduce-scatter.2.cloned.1.call-done = bf16[32,4096]{1,0:T(8,128)(2,1)} async-done(((bf16[512,4096]{1,0:T(8,128)(2,1)}), bf16[32,4096]{1,0:T(8,128)(2,1)}) %reduce-scatter.2.cloned.1.call-update) | async-done | bytes 262160 | tf_op jit(solution)/shard_map/reduce_scatter | solution.py:74
  170.2 1.8 reshape.45
  171.9 5.1 %all-to-all-start.1 = ((bf16[8,4,4096]{2,1,0:T(4,128)(2,1)}), bf16[8,4,4096]{2,1,0:T(4,128)(2,1)S(1)}, u32[]{:S(2)}, u32[]{:S(2)}) async-start(bf16[8,4,4096]{2,1,0:T(4,128)(2,1)} %reshape.45), calls=%async_computation.2 | async-start | bytes 524288 | tf_op jit(solution)/shard_map/all_to_all | solution.py:75
  177.0 4.5 %fusion.8 = (bf16[2048,512]{1,0:T(8,128)(2,1)}, bf16[2048,512]{1,0:T(8,128)(2,1)}) fusion(bf16[2048,1024]{1,0:T(8,128)(2,1)} %add_convert_fusion), kind=kLoop, calls=%fused_computation.24 | loop fusion | bytes 8388608 | tf_op jit(solution)/shard_map/slice | solution.py:87
  181.5 2.4 %all-to-all-done.1 = bf16[8,4,4096]{2,1,0:T(4,128)(2,1)S(1)} async-done(((bf16[8,4,4096]{2,1,0:T(4,128)(2,1)}), bf16[8,4,4096]{2,1,0:T(4,128)(2,1)S(1)}, u32[]{:S(2)}, u32[]{:S(2)}) %all-to-all-start.1) | async-done | bytes 262176 | tf_op jit(solution)/shard_map/all_to_all | solution.py:75
  183.9 0.1 reshape.46
  184.0 0.8 convolution_convert_fusion.1
  (6 shorter events, 0.0 us)
Async XLA Ops:
  7.2 2.2 %copy-start = (bf16[16,4096]{1,0:T(8,128)(2,1)S(1)}, bf16[16,4096]{1,0:T(8,128)(2,1)}, u32[]{:S(2)}) copy-start(bf16[16,4096]{1,0:T(8,128)(2,1)} %param.5) | copy-start | bytes 393220
  7.2 58.4 %all-gather.3.cloned.1.call-start = ((), (), s32[]{:S(2)}) async-start(), calls=%async_computation.3 | async-start | bytes 4456448 | tf_op jit(solution)/shard_map/all_gather | solution.py:51
  22.6 83.4 %all-gather.5.cloned.1.call-start = ((), (), s32[]{:S(2)}) async-start(), calls=%async_computation.5 | async-start | bytes 2228224 | tf_op jit(solution)/shard_map/all_gather | solution.py:52
  23.5 6.6 %collective-permute-start = (bf16[32,2048]{1,0:T(8,128)(2,1)S(1)}, bf16[32,2048]{1,0:T(8,128)(2,1)S(1)}, u32[]{:S(2)}, u32[]{:S(2)}) collective-permute-start(bf16[32,2048]{1,0:T(8,128)(2,1)S(1)} %constant_dynamic-slice_fusion), channel_id=1, source_target_pairs={{0,128},{128,0},{1,129},{129,1},{2,130},{130,2},{3,131},{131,3},{4... | collective-permute-start | bytes 393224 | tf_op jit(solution)/shard_map/ppermute | solution.py:30
  30.1 0.7 copy-start.3
  30.8 139.4 %reduce-scatter.2.cloned.1.call-start = ((), (), s32[]{:S(2)}) async-start(), calls=%async_computation.4 | async-start | bytes 4456448 | tf_op jit(solution)/shard_map/reduce_scatter | solution.py:74
  65.5 6.1 %copy-start.2 = (bf16[4096,512]{1,0:T(8,128)(2,1)S(1)}, bf16[4096,512]{1,0:T(8,128)(2,1)}, u32[]{:S(2)}) copy-start(bf16[4096,512]{1,0:T(8,128)(2,1)} %param.9) | copy-start | bytes 12582916
  65.5 6.2 %copy-start.4 = (bf16[512,4096]{1,0:T(8,128)(2,1)S(1)}, bf16[512,4096]{1,0:T(8,128)(2,1)}, u32[]{:S(2)}) copy-start(bf16[512,4096]{1,0:T(8,128)(2,1)} %all-gather.3.cloned.1.call-done) | copy-start | bytes 12582916
  71.7 2.6 %copy-start.1 = (bf16[4096,512]{1,0:T(8,128)(2,1)S(1)}, bf16[4096,512]{1,0:T(8,128)(2,1)}, u32[]{:S(2)}) copy-start(bf16[4096,512]{1,0:T(8,128)(2,1)} %param.8) | copy-start | bytes 12582916
  81.3 27.1 %collective-permute-start.1 = (bf16[512,1024]{0,1:T(8,128)(2,1)S(1)}, bf16[512,1024]{0,1:T(8,128)(2,1)S(1)}, u32[]{:S(2)}, u32[]{:S(2)}) collective-permute-start(bf16[512,1024]{0,1:T(8,128)(2,1)S(1)} %pad_maximum_fusion), channel_id=1, source_target_pairs={{0,128},{128,0},{1,129},{129,1},{2,130},{130,2},{3,131},{131,3},{4... | collective-permute-start | bytes 3145736 | tf_op jit(solution)/shard_map/ppermute | solution.py:30
  171.9 12.0 %all-to-all-start.1 = ((bf16[8,4,4096]{2,1,0:T(4,128)(2,1)}), bf16[8,4,4096]{2,1,0:T(4,128)(2,1)S(1)}, u32[]{:S(2)}, u32[]{:S(2)}) async-start(bf16[8,4,4096]{2,1,0:T(4,128)(2,1)} %reshape.45), calls=%async_computation.2 | async-start | bytes 524288 | tf_op jit(solution)/shard_map/all_to_all | solution.py:75
Sparse Core Ops, SparseCore 0:
  22.7 42.8 all-gather.2
  67.9 37.9 all-gather.4
  108.5 61.5 reduce-scatter.1
where the time goes:
time: 192 us; the launch traced here: 191 us
  waiting for transfers between devices  116 us (60%)
  matrix products  29.9 us (16%)
  between operations  13.9 us (7%)
  local copies, waits for them, and re-layouts  12 us (6%)
  blocking collectives  12 us (6%)
  starting transfers between devices  6.69 us (3%)
    reduce_scatter x1, waiting for transfers between devices, per_device(): lax.psum_scatter(partial_value, 's', scatter_dimension=0, tiled=True)  54.6 us
    all_gather x1, waiting for transfers between devices, per_device(): rows = lax.all_gather(mine, 's', axis=0, tiled=True)  32.5 us
    all_gather x1, waiting for transfers between devices, per_device(): far_rows = lax.all_gather(far_mine, 's', axis=0, tiled=True)  17.9 us
    dot_general x2, matrix products, contract_rows(): lax.dot_general(left_rows, right_rows, (((0,), (0,)), ((), ())), preferre...  13.2 us
    all_to_all x1, blocking collectives, per_device(): lax.all_to_all(outgoing.reshape(EXPERTS, CAP, model_width), 'e', split_ax...  12 us
    ppermute x2, waiting for transfers between devices, swap_dp(): return lax.ppermute(block, 'dp', [(0, 1), (1, 0)])  8.23 us
    dot_general x1, matrix products, per_device(): gate_pre = jnp.dot(rows, gate_weight, preferred_element_type=jnp.float32)  6.13 us
    all_to_all x1, starting transfers between devices, per_device(): lax.all_to_all(summed.reshape(EXPERTS, CAP, model_width), 'e', split_axis...  5.07 us
  transfers between devices with their start and end apart: 6, of which 6 were waited for; matrix products, arithmetic and copies ran while one was open for 19% of the time, Pallas kernels for 0%

commit v1 on v0

--- a/solution.py
+++ b/solution.py
@@ -48,7 +48,9 @@
         outgoing.reshape(EXPERTS, CAP, model_width), "e", split_axis=0, concat_axis=0, tiled=True
     ).reshape(EXPERTS * CAP, model_width)
     far_mine = swap_dp(lax.dynamic_slice_in_dim(mine, (1 - replica) * half, half, 1))
-    rows = lax.all_gather(mine, "s", axis=0, tiled=True)
+    rows = jnp.concatenate(
+        lax.all_to_all(jnp.stack([mine] * lax.axis_size("s")), "s", 0, 0), axis=0
+    )
     far_rows = lax.all_gather(far_mine, "s", axis=0, tiled=True)
     grad_h = (
         hidden_grad.reshape(EXPERTS, shards, CAP, ffd)

time: 192 us -> 238 us (1.24)
  waiting for transfers between devices: 116 us -> 150 us
  starting transfers between devices: 6.69 us -> 15.6 us
  matrix products: 29.9 us -> 32.3 us
    all_to_all x0 -> x1, waiting for transfers between devices: none -> 94.8 us  [per_device(): lax.all_to_all(jnp.stack([mine] * lax.axis_size('s')), 's', 0, 0)]
    all_gather x1 -> x0, waiting for transfers between devices: 32.5 us -> none  [per_device(): rows = lax.all_gather(mine, 's', axis=0, tiled=True)]
    reduce_scatter x1, waiting for transfers between devices: 54.6 us -> 26.7 us  [per_device(): lax.psum_scatter(partial_value, 's', scatter_dimension=0, tiled=True)]
    ppermute x2, waiting for transfers between devices: 8.23 us -> 26.2 us  [swap_dp(): return lax.ppermute(block, 'dp', [(0, 1), (1, 0)])]
    all_gather x1, waiting for transfers between devices: 17.9 us -> 0.01 us  [per_device(): far_rows = lax.all_gather(far_mine, 's', axis=0, tiled=True)]
    all_to_all x0 -> x1, starting transfers between devices: none -> 8.75 us  [per_device(): lax.all_to_all(jnp.stack([mine] * lax.axis_size('s')), 's', 0, 0)]
    another operation x0 -> x2, local copies, waits for them, and re-layouts: none -> 2.51 us  [per_device(): jnp.stack([mine] * lax.axis_size('s'))]
  transfers between devices with their start and end apart: 6 -> 6, of which waited for: 6 -> 5; matrix products, arithmetic and copies ran while one was open for 19% -> 16% of each run, Pallas kernels for 0% -> 0%
where the time goes in v1:
time: 238 us; the launch traced here: 237 us
  waiting for transfers between devices  150 us (63%)
  matrix products  32.3 us (14%)
  starting transfers between devices  15.6 us (7%)
  between operations  14.2 us (6%)
  blocking collectives  12 us (5%)
  local copies, waits for them, and re-layouts  11.8 us (5%)
    all_to_all x1, waiting for transfers between devices, per_device(): lax.all_to_all(jnp.stack([mine] * lax.axis_size('s')), 's', 0, 0)  94.8 us
    reduce_scatter x1, waiting for transfers between devices, per_device(): lax.psum_scatter(partial_value, 's', scatter_dimension=0, tiled=True)  26.7 us
    ppermute x2, waiting for transfers between devices, swap_dp(): return lax.ppermute(block, 'dp', [(0, 1), (1, 0)])  26.2 us
    dot_general x2, matrix products, contract_rows(): lax.dot_general(left_rows, right_rows, (((0,), (0,)), ((), ())), preferre...  13.3 us
    all_to_all x1, blocking collectives, per_device(): lax.all_to_all(outgoing.reshape(EXPERTS, CAP, model_width), 'e', split_ax...  12 us
    all_to_all x1, starting transfers between devices, per_device(): lax.all_to_all(jnp.stack([mine] * lax.axis_size('s')), 's', 0, 0)  8.75 us
    dot_general x1, matrix products, per_device(): gate_pre = jnp.dot(rows, gate_weight, preferred_element_type=jnp.float32)  6.12 us
    all_to_all x1, starting transfers between devices, per_device(): lax.all_to_all(summed.reshape(EXPERTS, CAP, model_width), 'e', split_axis...  5.21 us
  transfers between devices with their start and end apart: 6, of which 5 were waited for; matrix products, arithmetic and copies ran while one was open for 16% of the time, Pallas kernels for 0%

profile of v1, /device:TPU:16, one launch (start us, length us, event | category | flops | bytes accessed | tf_op | source)
XLA Modules:
  0.0 237.3 jit_solution(11352975598300916793)
XLA Ops:
  7.2 0.0 copy-start
  7.2 0.8 copy.25
  8.0 0.1 eq.29
  8.1 0.1 fusion.4
  8.1 0.1 reduce_window_sum.11
  8.2 0.2 select_reduce_fusion
  8.4 0.1 reduce_sum.21
  8.5 0.1 copy.26
  8.5 0.7 multiply_add_fusion
  9.2 0.1 convert_reduce_fusion
  9.3 0.0 copy-done
  9.3 0.2 convolution_convert_fusion
  9.6 0.1 reshape.46
  9.7 12.0 %all_to_all.15 = bf16[8,4,4096]{2,1,0:T(4,128)(2,1)S(1)} all-to-all(bf16[8,4,4096]{2,1,0:T(4,128)(2,1)S(1)} %reshape.46), channel_id=1, replica_groups=mesh['dp'=2,'e'=8,'s'=16] {'e'}, dimensions={0} | all-to-all | bytes 524288 | tf_op jit(solution)/shard_map/all_to_all | solution.py:47
  21.7 0.1 stack_reshape.2
  21.8 2.5 %stack.3 = bf16[16,32,4096]{2,1,0:T(8,128)(2,1)} broadcast(bf16[32,4096]{1,0:T(8,128)(2,1)S(1)} %stack_reshape.2), dimensions={1,2} | broadcast | bytes 4456448 | tf_op jit(solution)/shard_map/stack | solution.py:52
  24.2 8.8 %all-to-all-start.1 = ((bf16[16,32,4096]{2,1,0:T(8,128)(2,1)}), bf16[16,32,4096]{2,1,0:T(8,128)(2,1)}, u32[]{:S(2)}, u32[]{:S(2)}) async-start(bf16[16,32,4096]{2,1,0:T(8,128)(2,1)} %stack.3), calls=%async_computation.1 | async-start | bytes 8388608 | tf_op jit(solution)/shard_map/all_to_all | solution.py:52
  33.0 0.0 all-gather.2.cloned.1.call-start
  33.1 0.7 collective-permute-start
  33.8 6.6 %collective-permute-done = bf16[32,2048]{1,0:T(8,128)(2,1)S(1)} collective-permute-done((bf16[32,2048]{1,0:T(8,128)(2,1)S(1)}, bf16[32,2048]{1,0:T(8,128)(2,1)S(1)}, u32[]{:S(2)}, u32[]{:S(2)}) %collective-permute-start) | collective-permute-done | bytes 131104 | tf_op jit(solution)/shard_map/ppermute | solution.py:30
  40.4 0.7 copy-done.4
  41.1 0.0 all-gather.2.cloned.1.call-update
  41.1 0.0 reduce-scatter.2.cloned.1.call-start
  41.2 0.0 copy-done.3
  41.2 0.3 reshape.51
  41.5 0.1 copy.31
  41.6 0.4 reshape.50
  42.0 0.3 copy.28
  42.3 94.8 %all-to-all-done.1 = bf16[16,32,4096]{2,1,0:T(8,128)(2,1)} async-done(((bf16[16,32,4096]{2,1,0:T(8,128)(2,1)}), bf16[16,32,4096]{2,1,0:T(8,128)(2,1)}, u32[]{:S(2)}, u32[]{:S(2)}) %all-to-all-start.1) | async-done | bytes 4194336 | tf_op jit(solution)/shard_map/all_to_all | solution.py:52
  137.2 6.1 %multiply_convert_fusion = (bf16[512,512]{0,1:T(8,128)(2,1)S(1)}, f32[512,512]{0,1:T(8,128)S(1)}) fusion(f32[512,512]{0,1:T(8,128)S(1)} %copy.28, bf16[512,4096]{1,0:T(8,128)(2,1)} %bitcast.1, bf16[4096,512]{1,0:T(8,128)(2,1)} %param.8), kind=kOutput, calls=%fused_computation.12 | convolution fusion | flops 2149056512 | bytes 11010048 | tf_op jit(solution)/shard_map/dot_general | solution.py:61
  143.3 0.0 copy-start.1
  143.3 5.0 %fusion.3 = bf16[512,512]{0,1:T(8,128)(2,1)S(1)} fusion(f32[512,512]{0,1:T(8,128)S(1)} %copy.28, bf16[512,4096]{1,0:T(8,128)(2,1)} %bitcast.1, bf16[4096,512]{1,0:T(8,128)(2,1)S(1)} %copy-done.2, f32[512,512]{0,1:T(8,128)S(1)} %get-tuple-element.6), kind=kOutput, calls=%fused_computation.9 | convolution fusion | flops 2150105088 | bytes 11010048 | tf_op jit(solution)/shard_map/dot_general | solution.py:62
  148.3 0.0 copy-done.1
  148.3 2.4 %fusion.9 = f32[512,4096]{1,0:T(8,128)S(1)} fusion(bf16[512,512]{0,1:T(8,128)(2,1)S(1)} %fusion.3, bf16[4096,512]{1,0:T(8,128)(2,1)S(1)} %copy-done.1), kind=kOutput, calls=%fused_computation.25 | convolution fusion | flops 2147483648 | bytes 13107200 | tf_op jit(solution)/shard_map/dot_general | solution.py:69
  150.7 4.5 %add_convert_fusion.1 = bf16[512,4096]{1,0:T(8,128)(2,1)} fusion(f32[512,4096]{1,0:T(8,128)S(1)} %fusion.9, bf16[512,512]{0,1:T(8,128)(2,1)S(1)} %get-tuple-element.5, bf16[4096,512]{1,0:T(8,128)(2,1)S(1)} %copy-done.2), kind=kOutput, calls=%fused_computation.1 | convolution fusion | flops 2151677952 | bytes 17301504 | tf_op jit(solution)/shard_map/dot_general | solution.py:72
  155.2 0.0 reduce-scatter.2.cloned.1.call-update
  155.2 0.1 pad_maximum_fusion
  155.3 0.9 collective-permute-start.1
  156.2 6.0 %convolution_convert_fusion.2 = bf16[2048,1024]{1,0:T(8,128)(2,1)} fusion(bf16[512,4096]{1,0:T(8,128)(2,1)} %bitcast.1, s32[]{:T(128)S(6)} %select_n.6, bf16[512,512]{0,1:T(8,128)(2,1)S(1)} %get-tuple-element.5, bf16[512,512]{0,1:T(8,128)(2,1)S(1)} %fusion.3), kind=kOutput, calls=%fused_computation.4 | convolution fusion | flops 2151677952 | bytes 7340036 | tf_op jit(solution)/shard_map/dot_general | solution.py:24
  162.1 19.5 %collective-permute-done.1 = bf16[512,1024]{0,1:T(8,128)(2,1)S(1)} collective-permute-done((bf16[512,1024]{0,1:T(8,128)(2,1)S(1)}, bf16[512,1024]{0,1:T(8,128)(2,1)S(1)}, u32[]{:S(2)}, u32[]{:S(2)}) %collective-permute-start.1) | collective-permute-done | bytes 1048608 | tf_op jit(solution)/shard_map/ppermute | solution.py:30
  181.6 7.3 %add_convert_fusion = bf16[2048,1024]{1,0:T(8,128)(2,1)} fusion(bf16[2048,1024]{1,0:T(8,128)(2,1)} %convolution_convert_fusion.2, bf16[512,2048]{1,0:T(8,128)(2,1)} %all-gather.2.cloned.1.call-done, bf16[512,1024]{0,1:T(8,128)(2,1)S(1)} %collective-permute-done.1), kind=kOutput, calls=%fused_computation | convolution fusion | flops 2153775104 | bytes 11534336 | tf_op jit(solution)/shard_map/dot_general | solution.py:24
  188.9 26.7 %reduce-scatter.2.cloned.1.call-done = bf16[32,4096]{1,0:T(8,128)(2,1)} async-done(((bf16[512,4096]{1,0:T(8,128)(2,1)}), bf16[32,4096]{1,0:T(8,128)(2,1)}) %reduce-scatter.2.cloned.1.call-update) | async-done | bytes 262160 | tf_op jit(solution)/shard_map/reduce_scatter | solution.py:76
  215.7 1.8 reshape.48
  217.4 5.2 %all-to-all-start.2 = ((bf16[8,4,4096]{2,1,0:T(4,128)(2,1)}), bf16[8,4,4096]{2,1,0:T(4,128)(2,1)S(1)}, u32[]{:S(2)}, u32[]{:S(2)}) async-start(bf16[8,4,4096]{2,1,0:T(4,128)(2,1)} %reshape.48), calls=%async_computation.3 | async-start | bytes 524288 | tf_op jit(solution)/shard_map/all_to_all | solution.py:77
  222.6 4.5 %fusion.8 = (bf16[2048,512]{1,0:T(8,128)(2,1)}, bf16[2048,512]{1,0:T(8,128)(2,1)}) fusion(bf16[2048,1024]{1,0:T(8,128)(2,1)} %add_convert_fusion), kind=kLoop, calls=%fused_computation.24 | loop fusion | bytes 8388608 | tf_op jit(solution)/shard_map/slice | solution.py:89
  227.1 2.4 %all-to-all-done.2 = bf16[8,4,4096]{2,1,0:T(4,128)(2,1)S(1)} async-done(((bf16[8,4,4096]{2,1,0:T(4,128)(2,1)}), bf16[8,4,4096]{2,1,0:T(4,128)(2,1)S(1)}, u32[]{:S(2)}, u32[]{:S(2)}) %all-to-all-start.2) | async-done | bytes 262176 | tf_op jit(solution)/shard_map/all_to_all | solution.py:77
  229.6 0.1 reshape.49
  229.6 0.8 convolution_convert_fusion.1
  (6 shorter events, 0.0 us)
Async XLA Ops:
  7.2 2.2 copy-start
  24.2 16.9 %copy-start.3 = (bf16[512,512]{1,0:T(8,128)(2,1)S(1)}, bf16[512,512]{1,0:T(8,128)(2,1)}, u32[]{:S(2)}) copy-start(bf16[512,512]{1,0:T(8,128)(2,1)} %param.7) | copy-start | bytes 1572868
  24.2 112.9 %all-to-all-start.1 = ((bf16[16,32,4096]{2,1,0:T(8,128)(2,1)}), bf16[16,32,4096]{2,1,0:T(8,128)(2,1)}, u32[]{:S(2)}, u32[]{:S(2)}) async-start(bf16[16,32,4096]{2,1,0:T(8,128)(2,1)} %stack.3), calls=%async_computation.1 | async-start | bytes 8388608 | tf_op jit(solution)/shard_map/all_to_all | solution.py:52
  33.0 129.1 %all-gather.2.cloned.1.call-start = ((), (), s32[]{:S(2)}) async-start(), calls=%async_computation.5 | async-start | bytes 2228224 | tf_op jit(solution)/shard_map/all_gather | solution.py:54
  33.1 7.3 %collective-permute-start = (bf16[32,2048]{1,0:T(8,128)(2,1)S(1)}, bf16[32,2048]{1,0:T(8,128)(2,1)S(1)}, u32[]{:S(2)}, u32[]{:S(2)}) collective-permute-start(bf16[32,2048]{1,0:T(8,128)(2,1)S(1)} %constant_dynamic-slice_fusion), channel_id=1, source_target_pairs={{0,128},{128,0},{1,129},{129,1},{2,130},{130,2},{3,131},{131,3},{4... | collective-permute-start | bytes 393224 | tf_op jit(solution)/shard_map/ppermute | solution.py:30
  40.4 0.7 copy-start.4
  41.1 174.5 %reduce-scatter.2.cloned.1.call-start = ((), (), s32[]{:S(2)}) async-start(), calls=%async_computation.4 | async-start | bytes 4456448 | tf_op jit(solution)/shard_map/reduce_scatter | solution.py:76
  137.2 6.1 %copy-start.2 = (bf16[4096,512]{1,0:T(8,128)(2,1)S(1)}, bf16[4096,512]{1,0:T(8,128)(2,1)}, u32[]{:S(2)}) copy-start(bf16[4096,512]{1,0:T(8,128)(2,1)} %param.9) | copy-start | bytes 12582916
  143.3 5.0 %copy-start.1 = (bf16[4096,512]{1,0:T(8,128)(2,1)S(1)}, bf16[4096,512]{1,0:T(8,128)(2,1)}, u32[]{:S(2)}) copy-start(bf16[4096,512]{1,0:T(8,128)(2,1)} %param.8) | copy-start | bytes 12582916
  155.3 26.4 %collective-permute-start.1 = (bf16[512,1024]{0,1:T(8,128)(2,1)S(1)}, bf16[512,1024]{0,1:T(8,128)(2,1)S(1)}, u32[]{:S(2)}, u32[]{:S(2)}) collective-permute-start(bf16[512,1024]{0,1:T(8,128)(2,1)S(1)} %pad_maximum_fusion), channel_id=1, source_target_pairs={{0,128},{128,0},{1,129},{129,1},{2,130},{130,2},{3,131},{131,3},{4... | collective-permute-start | bytes 3145736 | tf_op jit(solution)/shard_map/ppermute | solution.py:30
  217.4 12.1 %all-to-all-start.2 = ((bf16[8,4,4096]{2,1,0:T(4,128)(2,1)}), bf16[8,4,4096]{2,1,0:T(4,128)(2,1)S(1)}, u32[]{:S(2)}, u32[]{:S(2)}) async-start(bf16[8,4,4096]{2,1,0:T(4,128)(2,1)} %reshape.48), calls=%async_computation.3 | async-start | bytes 524288 | tf_op jit(solution)/shard_map/all_to_all | solution.py:77
Sparse Core Ops, SparseCore 0:
  41.2 63.0 all-gather.1
  155.3 60.3 reduce-scatter.1
